TPU v7x, 256 devices: a whole 4x4x8 slice. The times are simulated.
256 devices in a mesh: gx: 4 (over x), gy: 8 (over z), gz: 8 (over y, core).
Axes of the slice: x: 4, y: 4, z: 8, core: 2. Of those that a mesh axis runs over, the one named last changes fastest.
Arguments:
- patch_fields: bfloat16 [8192, 4, 32768], P(('gx', 'gy', 'gz')), may hold values from -54 to 54
- slot_snapshot: int32 [8192], P(('gx', 'gy', 'gz')), may hold values from -1 to 15, as said below
- slot_brick: int32 [8192], P(('gx', 'gy', 'gz')), may hold values from -1 to 255, as said below
- prior_basis: float32 [64, 32], replicated, may hold values from -0.75 to 0.75
Outputs:
- gram_matrix: float32 [64, 64], replicated
- mode_fields: bfloat16 [64, 128, 4096], P('gx', 'gy', 'gz')
- diffused: bfloat16 [64, 128, 4096], P('gx', 'gy', 'gz')
- reduced: float32 [32, 32], replicated
Inputs may be any that keep to these rules, and one draw needn't show every extreme that they name: `slot_snapshot`: -1 marks an empty slot; on every device the live slots come first, and some device has all 32 slots live. `slot_brick`: a brick is named by its device index in the order gx, gy, gz with gz fastest; -1 exactly where slot_snapshot is -1; every pair of a snapshot and a brick is held by exactly one slot; a patch's owner has the same gz index as its brick; no device holds more than 1 patches of one brick, a bound reached in every gz plane.
All inputs are finite; a program needn't handle non-finite values.
Results may differ from a plain program's by a relative error of at most 0.0076.
Values may be sent and summed in bfloat16 or wider, within the bound.
A program may use at most 128 MiB of HBM per device.

v0:
```python
import jax
import jax.numpy as jnp
from jax import lax
from jax.sharding import Mesh
from jax.sharding import PartitionSpec as P

SNAPS = 16
FIELDS = 4
PATCH = 32
MODES = 32
EDGE = 16
CELLS = 4096
COLS = 64
GZ = ("gz_0", "gz_1")
GX_GY_GZ = ("gx", "gy", "gz_0", "gz_1")
HIGHEST = lax.Precision.HIGHEST


def extended(value, sides, width):
    edges = {}
    for axis, dim in sides:
        devices, length = (lax.axis_size(axis), value.shape[dim])
        up = [(i, (i + 1) % devices) for i in range(devices - 1)]
        last = lax.slice_in_dim(value, length - width, length, axis=dim)
        first = lax.slice_in_dim(value, 0, width, axis=dim)
        edges[dim] = (
            lax.ppermute(last, axis, up),
            lax.ppermute(first, axis, [(b, a) for a, b in up]),
        )
    done = []
    for _, dim in sides:
        low, high = edges[dim]
        around = [(width, width) if d in done else (0, 0) for d in range(value.ndim)]
        value = jnp.concatenate([jnp.pad(low, around), value, jnp.pad(high, around)], axis=dim)
        done.append(dim)
    return value


def extended_2(value, sides, width):
    for axis, dim in sides:
        devices, length = (lax.axis_size(axis), value.shape[dim])
        up = [(i, (i + 1) % devices) for i in range(devices - 1)]
        down = [(j, i) for i, j in up]
        last = lax.slice_in_dim(value, length - width, length, axis=dim)
        first = lax.slice_in_dim(value, 0, width, axis=dim)
        before = lax.ppermute(last, axis, up)
        after = lax.ppermute(first, axis, down)
        value = jnp.concatenate([before, value, after], axis=dim)
    return value


def over_axes(value, axes):
    for axis in axes:
        value = lax.psum(value, axis)
    return value


def average_cells(fine_data):
    row_count = fine_data.shape[0]
    view = fine_data.reshape(row_count * FIELDS * EDGE, 2, EDGE, 2 * PATCH)
    pair_x = view[:, 0].astype(jnp.float32) + view[:, 1].astype(jnp.float32)
    pair_y = pair_x[:, :, :PATCH] + pair_x[:, :, PATCH:]
    pairing = (
        jnp.arange(PATCH, dtype=jnp.int32)[:, None] // 2
        == jnp.arange(EDGE, dtype=jnp.int32)[None, :]
    ).astype(jnp.float32) * 0.125
    means = jnp.dot(pair_y.reshape(-1, PATCH), pairing, precision=HIGHEST)
    return means.reshape(row_count, FIELDS, CELLS).astype(jnp.bfloat16)


def seven_point(center, around_xy, around_z, stride):
    total = around_xy[2:, 1:-1] + around_xy[:-2, 1:-1] + around_xy[1:-1, 2:] + around_xy[1:-1, :-2]
    total = total + around_z[:, :, 2 * stride :] + around_z[:, :, : -2 * stride]
    return total - 6.0 * center


def factor_basis(gram_matrix, prior_basis):
    lower_factor = jnp.linalg.cholesky(gram_matrix)
    return lax.linalg.triangular_solve(
        lower_factor, prior_basis, left_side=True, lower=True, transpose_a=True
    )


def shards(patch_fields, slot_snapshot, slot_brick, prior_basis):
    size_x = lax.axis_size("gx")
    size_y = lax.axis_size("gy")
    size_z = lax.axis_size(GZ)
    plane_size = size_x * size_y
    slot_count = slot_snapshot.shape[0]
    pair_depth = slot_count // plane_size
    total_cells = CELLS * plane_size * size_z
    is_live = slot_snapshot >= 0
    slot_ids = jnp.arange(slot_count, dtype=jnp.int32)
    target_peer = jnp.where(is_live, slot_brick // size_z, plane_size)
    earlier = (target_peer[:, None] == target_peer[None, :]) & (
        slot_ids[None, :] < slot_ids[:, None]
    )
    pair_rank = jnp.sum(earlier.astype(jnp.int32), axis=1)
    position = jnp.where(is_live, target_peer * pair_depth + pair_rank, slot_count)
    slot_hits = position[:, None] == slot_ids[None, :]
    filled = jnp.any(slot_hits, axis=0)
    source = jnp.sum(jnp.where(slot_hits, slot_ids[:, None], 0), axis=0)
    sent_snapshot = jnp.where(filled, jnp.take(slot_snapshot, source), -1)
    payload = jnp.take(average_cells(patch_fields), source, axis=0)
    received, received_snapshot = (
        lax.all_to_all(payload, ("gx", "gy"), split_axis=0, concat_axis=0, tiled=True),
        lax.all_to_all(sent_snapshot, ("gx", "gy"), split_axis=0, concat_axis=0, tiled=True),
    )
    snapshots = jnp.arange(SNAPS, dtype=jnp.int32)
    chosen = jnp.sum(
        jnp.where(received_snapshot[None, :] == snapshots[:, None], slot_ids[None, :], 0), axis=1
    )
    arrived = jnp.take(received, chosen, axis=0)
    columns = arrived.reshape(COLS, CELLS)
    partial_gram = jnp.dot(columns, columns.T, preferred_element_type=jnp.float32)
    data_wide = columns.astype(jnp.float32).T
    data_block = columns.T.reshape(EDGE, EDGE, EDGE * COLS)
    data_xy = extended(data_block, (("gx", 0), ("gy", 1)), 1).astype(jnp.float32)
    data_z = extended_2(data_block, ((GZ, 2),), COLS).astype(jnp.float32)
    data_image = seven_point(data_block.astype(jnp.float32), data_xy, data_z, COLS).reshape(
        CELLS, COLS
    )
    partial_cross = jnp.dot(data_wide.T, data_image, precision=HIGHEST)
    gram_total, cross_total = (
        over_axes(partial_gram, GX_GY_GZ),
        over_axes(partial_cross, GX_GY_GZ),
    )
    gram_matrix = gram_total / total_cells
    coeffs = factor_basis(gram_matrix, prior_basis)
    mode_basis = jnp.dot(data_wide, coeffs, precision=HIGHEST)
    mode_image = jnp.dot(data_image, coeffs, precision=HIGHEST)
    inner = jnp.dot(cross_total / total_cells, coeffs, precision=HIGHEST)
    reduced = jnp.dot(coeffs.T, inner, precision=HIGHEST)
    mode_fields = mode_basis.reshape(EDGE, EDGE, EDGE * MODES).astype(jnp.bfloat16)
    diffused = mode_image.reshape(EDGE, EDGE, EDGE * MODES).astype(jnp.bfloat16)
    return (gram_matrix, mode_fields, diffused, reduced)


def solution(mesh):
    split = Mesh(
        mesh.devices.reshape(mesh.shape["gx"], mesh.shape["gy"], 4, 2), ("gx", "gy", "gz_0", "gz_1")
    )
    in_specs = (P(GX_GY_GZ, None, None), P(GX_GY_GZ), P(GX_GY_GZ), P())
    out_specs = (P(), P("gx", "gy", GZ), P("gx", "gy", GZ), P())
    return jax.shard_map(
        shards, mesh=split, in_specs=in_specs, out_specs=out_specs, check_vma=False
    )
```

profile of v0, /device:TPU:1, one launch (start us, length us, event | category | flops | bytes accessed | tf_op | source)
XLA Modules:
  0.0 251.8 jit_solution(11054224175543935289)
XLA Ops:
  2.4 1.4 gather_fusion
  4.4 11.9 %all-to-all-start = ((s32[32,1,1]{2,1,0:T(1,128)}), s32[32,1,1]{2,1,0:T(1,128)S(1)}, u32[]{:S(2)}, u32[]{:S(2)}) async-start(s32[32,1,1]{2,1,0:T(1,128)} %copy.36), calls=%async_computation | async-start | bytes 32768 | tf_op jit(solution)/shard_map/all_to_all | solution.py:107
  16.3 27.2 %reshape.237 = bf16[2048,2,16,64]{3,2,1,0:T(8,128)(2,1)} reshape(bf16[32,4,32768]{2,1,0:T(4,128)(2,1)} %param.4) | data formatting | bytes 16777216 | tf_op jit(solution)/shard_map/reshape | solution.py:60
  43.6 6.9 %add_bitcast_fusion = f32[2048,16,64]{2,1,0:T(8,128)S(1)} fusion(bf16[2048,2,16,64]{3,2,1,0:T(8,128)(2,1)} %reshape.237), kind=kLoop, calls=%fused_computation.5 | loop fusion | flops 6291456 | bytes 16777216 | tf_op jit(solution)/shard_map/add | solution.py:61
  50.5 7.5 %slice_add_fusion = f32[2048,16,32]{2,1,0:T(8,128)} fusion(f32[2048,16,64]{2,1,0:T(8,128)S(1)} %add_bitcast_fusion), kind=kLoop, calls=%fused_computation.4 | loop fusion | flops 1048576 | bytes 12582912 | tf_op jit(solution)/shard_map/add | solution.py:62
  58.0 17.3 %convolution_convert_fusion = bf16[32768,16]{0,1:T(8,128)(2,1)S(1)} fusion(f32[32768,32]{1,0:T(8,128)} %bitcast.40, s32[32]{0:T(128)S(1)} %and_select_fusion), kind=kOutput, calls=%fused_computation.3 | convolution fusion | flops 201851904 | bytes 5243008 | tf_op jit(solution)/shard_map/dot_general | solution.py:67
  75.3 6.2 %copy.37 = bf16[32768,16]{1,0:T(8,128)(2,1)} copy(bf16[32768,16]{0,1:T(8,128)(2,1)S(1)} %convolution_convert_fusion) | data formatting | bytes 2097152 | tf_op jit(solution)/shard_map/convert_element_type | solution.py:68
  81.5 10.8 %convert_element_type.47 = bf16[32,4,4096]{2,1,0:T(4,128)(2,1)S(1)} reshape(bf16[32768,16]{1,0:T(8,128)(2,1)} %copy.37) | data formatting | bytes 2097152 | tf_op jit(solution)/shard_map/convert_element_type | solution.py:68
  92.2 1.4 gather_fusion.1
  93.7 1.6 broadcast_select_fusion
  95.3 9.4 %all-to-all-start.1 = ((bf16[32,4,4096]{2,1,0:T(4,128)(2,1)}), bf16[32,4,4096]{2,1,0:T(4,128)(2,1)S(1)}, u32[]{:S(2)}, u32[]{:S(2)}) async-start(bf16[32,4,4096]{2,1,0:T(4,128)(2,1)} %broadcast_select_fusion), calls=%async_computation.1 | async-start | bytes 2097152 | tf_op jit(solution)/shard_map/all_to_all | solution.py:106
  105.7 23.5 %all-to-all-done.1 = bf16[32,4,4096]{2,1,0:T(4,128)(2,1)S(1)} async-done(((bf16[32,4,4096]{2,1,0:T(4,128)(2,1)}), bf16[32,4,4096]{2,1,0:T(4,128)(2,1)S(1)}, u32[]{:S(2)}, u32[]{:S(2)}) %all-to-all-start.1) | async-done | bytes 1048608 | tf_op jit(solution)/shard_map/all_to_all | solution.py:106
  129.1 1.0 gather_fusion.2
  132.1 8.2 %collective-permute-start.4 = (bf16[16,16,64]{2,1,0:T(8,128)(2,1)S(1)}, bf16[16,16,64]{2,1,0:T(8,128)(2,1)S(1)}, u32[]{:S(2)}, u32[]{:S(2)}) collective-permute-start(bf16[16,16,64]{2,1,0:T(8,128)(2,1)S(1)} %get-tuple-element.37), channel_id=1, source_target_pairs={{0,1},{1,2},{2,3},{3,4},{4,5},{5,6},{6,7},{8,9},{9,10},{10,11},{11... | collective-permute-start | bytes 98312 | tf_op jit(solution)/shard_map/ppermute | solution.py:46
  140.5 1.9 collective-permute-start.5
  142.4 1.3 collective-permute-start.3
  143.7 4.0 %collective-permute-start = (bf16[16,1,1024]{2,1,0:T(2,128)(2,1)S(1)}, bf16[16,1,1024]{2,1,0:T(2,128)(2,1)S(1)}, u32[]{:S(2)}, u32[]{:S(2)}) collective-permute-start(bf16[16,1,1024]{2,1,0:T(2,128)(2,1)S(1)} %get-tuple-element.34), channel_id=1, source_target_pairs={{0,8},{8,16},{16,24},{24,32},{32,40},{40,48},{48,56},{1,9},{9,17},... | collective-permute-start | bytes 98312 | tf_op jit(solution)/shard_map/ppermute | solution.py:27
  147.8 1.3 collective-permute-start.2
  149.2 4.0 %collective-permute-start.1 = (bf16[1,16,1024]{2,1,0:T(8,128)(2,1)S(1)}, bf16[1,16,1024]{2,1,0:T(8,128)(2,1)S(1)}, u32[]{:S(2)}, u32[]{:S(2)}) collective-permute-start(bf16[1,16,1024]{2,1,0:T(8,128)(2,1)S(1)} %slice.70), channel_id=1, source_target_pairs={{0,64},{64,128},{128,192},{1,65},{65,129},{129,193},{2,66},{66,130... | collective-permute-start | bytes 98312 | tf_op jit(solution)/shard_map/ppermute | solution.py:27
  154.7 1.5 fusion.2
  156.1 1.7 reshape.240
  157.8 1.8 fusion.31
  159.6 13.5 %all-reduce.4 = (f32[64,64]{0,1:T(8,128)S(1)}, f32[64,64]{0,1:T(8,128)S(1)}) all-reduce(f32[64,64]{0,1:T(8,128)S(1)} %fusion.30, f32[64,64]{0,1:T(8,128)S(1)} %fusion.31), channel_id=1, replica_groups=mesh['gx'=4,'gy'=8,'gz_0'=4,'gz_1'=2] {'gx'}, use_global_device_ids=true, to_apply=%region_4.5 | all-reduce | flops 8192 | bytes 65536 | tf_op jit(solution)/shard_map/psum | solution.py:54
  173.1 21.7 %all-reduce.2 = (f32[64,64]{0,1:T(8,128)S(1)}, f32[64,64]{0,1:T(8,128)S(1)}) all-reduce(f32[64,64]{0,1:T(8,128)S(1)} %get-tuple-element.28, f32[64,64]{0,1:T(8,128)S(1)} %get-tuple-element.29), channel_id=1, replica_groups=mesh['gx'=4,'gy'=8,'gz_0'=4,'gz_1'=2] {'gy'}, use_global_device_ids=true, to_apply=%region_5.6 | all-reduce | flops 8192 | bytes 65536 | tf_op jit(solution)/shard_map/psum | solution.py:54
  194.8 13.0 %all-reduce.3 = (f32[64,64]{0,1:T(8,128)S(1)}, f32[64,64]{0,1:T(8,128)S(1)}) all-reduce(f32[64,64]{0,1:T(8,128)S(1)} %get-tuple-element.24, f32[64,64]{0,1:T(8,128)S(1)} %get-tuple-element.25), channel_id=1, replica_groups=mesh['gx'=4,'gy'=8,'gz_0'=4,'gz_1'=2] {'gz_0'}, use_global_device_ids=true, to_apply=%region_6.7 | all-reduce | flops 8192 | bytes 65536 | tf_op jit(solution)/shard_map/psum | solution.py:54
  207.9 21.5 %all-reduce.5 = (f32[64,64]{0,1:T(8,128)S(1)}, f32[64,64]{0,1:T(8,128)S(1)}) all-reduce(f32[64,64]{0,1:T(8,128)S(1)} %get-tuple-element.26, f32[64,64]{0,1:T(8,128)S(1)} %get-tuple-element.27), channel_id=1, replica_groups=mesh['gx'=4,'gy'=8,'gz_0'=4,'gz_1'=2] {'gz_1'}, use_global_device_ids=true, to_apply=%region_7.8 | all-reduce | flops 8192 | bytes 65536 | tf_op jit(solution)/shard_map/psum | solution.py:54
  229.6 5.8 %cholesky.16 = f32[64,64]{1,0:T(8,128)S(1)} custom-call(f32[64,64]{1,0:T(8,128)S(1)} %fusion.11), custom_call_target="Cholesky" | custom-call | tf_op jit(solution)/shard_map/jit(cholesky)/cholesky | solution.py:78
  236.7 4.9 %custom-call.6 = f32[1,64,64]{1,2,0:T(8,128)S(1)} custom-call(f32[1,64,64]{2,1,0:T(8,128)S(1)} %fusion.8), custom_call_target="InvertDiagBlocksLowerTriangular" | custom-call | tf_op jit(solution)/shard_map/triangular_solve | solution.py:79
  241.8 2.4 convolution_convert_fusion.2
  244.2 2.3 convolution_convert_fusion.1
  247.0 1.7 convert_element_type.49
  249.2 1.7 convert_element_type.54
  (57 shorter events, 10.5 us)
Async XLA Ops:
  0.6 241.0 %copy-start = (f32[64,32]{0,1:T(8,128)S(1)}, f32[64,32]{0,1:T(8,128)}, u32[]{:S(2)}) copy-start(f32[64,32]{0,1:T(8,128)} %param.7) | copy-start | bytes 24580
  4.4 90.8 %all-to-all-start = ((s32[32,1,1]{2,1,0:T(1,128)}), s32[32,1,1]{2,1,0:T(1,128)S(1)}, u32[]{:S(2)}, u32[]{:S(2)}) async-start(s32[32,1,1]{2,1,0:T(1,128)} %copy.36), calls=%async_computation | async-start | bytes 32768 | tf_op jit(solution)/shard_map/all_to_all | solution.py:107
  95.3 33.9 %all-to-all-start.1 = ((bf16[32,4,4096]{2,1,0:T(4,128)(2,1)}), bf16[32,4,4096]{2,1,0:T(4,128)(2,1)S(1)}, u32[]{:S(2)}, u32[]{:S(2)}) async-start(bf16[32,4,4096]{2,1,0:T(4,128)(2,1)} %broadcast_select_fusion), calls=%async_computation.1 | async-start | bytes 2097152 | tf_op jit(solution)/shard_map/all_to_all | solution.py:106
  131.1 1.1 copy-start.1
  132.1 17.1 %collective-permute-start.4 = (bf16[16,16,64]{2,1,0:T(8,128)(2,1)S(1)}, bf16[16,16,64]{2,1,0:T(8,128)(2,1)S(1)}, u32[]{:S(2)}, u32[]{:S(2)}) collective-permute-start(bf16[16,16,64]{2,1,0:T(8,128)(2,1)S(1)} %get-tuple-element.37), channel_id=1, source_target_pairs={{0,1},{1,2},{2,3},{3,4},{4,5},{5,6},{6,7},{8,9},{9,10},{10,11},{11... | collective-permute-start | bytes 98312 | tf_op jit(solution)/shard_map/ppermute | solution.py:46
  140.5 13.1 %collective-permute-start.5 = (bf16[16,16,64]{2,1,0:T(8,128)(2,1)S(1)}, bf16[16,16,64]{2,1,0:T(8,128)(2,1)S(1)}, u32[]{:S(2)}, u32[]{:S(2)}) collective-permute-start(bf16[16,16,64]{2,1,0:T(8,128)(2,1)S(1)} %get-tuple-element.36), channel_id=1, source_target_pairs={{1,0},{2,1},{3,2},{4,3},{5,4},{6,5},{7,6},{9,8},{10,9},{11,10},{12... | collective-permute-start | bytes 98312 | tf_op jit(solution)/shard_map/ppermute | solution.py:47
  142.4 11.8 %collective-permute-start.3 = (bf16[16,1,1024]{2,1,0:T(2,128)(2,1)S(1)}, bf16[16,1,1024]{2,1,0:T(2,128)(2,1)S(1)}, u32[]{:S(2)}, u32[]{:S(2)}) collective-permute-start(bf16[16,1,1024]{2,1,0:T(2,128)(2,1)S(1)} %get-tuple-element.35), channel_id=1, source_target_pairs={{8,0},{16,8},{24,16},{32,24},{40,32},{48,40},{56,48},{9,1},{17,9},... | collective-permute-start | bytes 98312 | tf_op jit(solution)/shard_map/ppermute | solution.py:28
  143.7 10.6 %collective-permute-start = (bf16[16,1,1024]{2,1,0:T(2,128)(2,1)S(1)}, bf16[16,1,1024]{2,1,0:T(2,128)(2,1)S(1)}, u32[]{:S(2)}, u32[]{:S(2)}) collective-permute-start(bf16[16,1,1024]{2,1,0:T(2,128)(2,1)S(1)} %get-tuple-element.34), channel_id=1, source_target_pairs={{0,8},{8,16},{16,24},{24,32},{32,40},{40,48},{48,56},{1,9},{9,17},... | collective-permute-start | bytes 98312 | tf_op jit(solution)/shard_map/ppermute | solution.py:27
  147.8 6.5 %collective-permute-start.2 = (bf16[1,16,1024]{2,1,0:T(8,128)(2,1)S(1)}, bf16[1,16,1024]{2,1,0:T(8,128)(2,1)S(1)}, u32[]{:S(2)}, u32[]{:S(2)}) collective-permute-start(bf16[1,16,1024]{2,1,0:T(8,128)(2,1)S(1)} %slice.72), channel_id=1, source_target_pairs={{64,0},{128,64},{192,128},{65,1},{129,65},{193,129},{66,2},{130,66... | collective-permute-start | bytes 98312 | tf_op jit(solution)/shard_map/ppermute | solution.py:28
  149.2 5.0 %collective-permute-start.1 = (bf16[1,16,1024]{2,1,0:T(8,128)(2,1)S(1)}, bf16[1,16,1024]{2,1,0:T(8,128)(2,1)S(1)}, u32[]{:S(2)}, u32[]{:S(2)}) collective-permute-start(bf16[1,16,1024]{2,1,0:T(8,128)(2,1)S(1)} %slice.70), channel_id=1, source_target_pairs={{0,64},{64,128},{128,192},{1,65},{65,129},{129,193},{2,66},{66,130... | collective-permute-start | bytes 98312 | tf_op jit(solution)/shard_map/ppermute | solution.py:27
  229.5 16.9 %copy-start.2 = (f32[64,64]{1,0:T(8,128)}, f32[64,64]{1,0:T(8,128)S(1)}, u32[]{:S(2)}) copy-start(f32[64,64]{1,0:T(8,128)S(1)} %copy.44) | copy-start | bytes 49156
where the time goes:
time: 253 us; the launch traced here: 252 us
  blocking collectives  69.8 us (28%)
  local copies, waits for them, and re-layouts  57.5 us (23%)
  starting transfers between devices  42 us (17%)
  other arithmetic  32.9 us (13%)
  matrix products  25.1 us (10%)
  waiting for transfers between devices  23.5 us (9%)
    psum x4, blocking collectives, over_axes(): value = lax.psum(value, axis)  69.8 us
    reshape x1, local copies, waits for them, and re-layouts, average_cells(): view = fine_data.reshape(row_count * FIELDS * EDGE, 2, EDGE, 2 * PATCH)  27.2 us
    all_to_all x1, waiting for transfers between devices, shards(): lax.all_to_all(payload, ('gx', 'gy'), split_axis=0, concat_axis=0, tiled=...  23.5 us
    dot_general x1, matrix products, average_cells(): means = jnp.dot(pair_y.reshape(-1, PATCH), pairing, precision=HIGHEST)  17.3 us
    convert_element_type x2, local copies, waits for them, and re-layouts, average_cells(): return means.reshape(row_count, FIELDS, CELLS).astype(jnp.bfloat16)  17 us
    all_to_all x1, starting transfers between devices, shards(): lax.all_to_all(sent_snapshot, ('gx', 'gy'), split_axis=0, concat_axis=0,...  11.9 us
    all_to_all x1, starting transfers between devices, shards(): lax.all_to_all(payload, ('gx', 'gy'), split_axis=0, concat_axis=0, tiled=...  9.4 us
    ppermute x1, starting transfers between devices, extended_2(): before = lax.ppermute(last, axis, up)  8.21 us
  transfers between devices with their start and end apart: 8, of which 1 were waited for; matrix products, arithmetic and copies ran while one was open for 32% of the time, Pallas kernels for 0%

commit v1 on v0

--- a/solution.py
+++ b/solution.py
@@ -51,7 +51,7 @@
 
 def over_axes(value, axes):
     for axis in axes:
-        value = lax.psum(value, axis)
+        value = jnp.sum(lax.all_gather(value, axis), axis=0)
     return value
 
 

time: 253 us -> 284 us (1.12)
  blocking collectives: 69.8 us -> 108 us
  starting transfers between devices: 42 us -> 37.1 us
    all_gather x0 -> x8, blocking collectives: none -> 108 us  [over_axes(): value = jnp.sum(lax.all_gather(value, axis), axis=0)]
    psum x4 -> x0, blocking collectives: 69.8 us -> none  [over_axes(): value = lax.psum(value, axis)]
    ppermute x1, starting transfers between devices: 8.21 us -> 3.15 us  [extended_2(): before = lax.ppermute(last, axis, up)]
  transfers between devices with their start and end apart: 8 -> 8, of which waited for: 1 -> 1; matrix products, arithmetic and copies ran while one was open for 32% -> 30% of each run, Pallas kernels for 0% -> 0%
where the time goes in v1:
time: 284 us; the launch traced here: 283 us
  blocking collectives  108 us (38%)
  local copies, waits for them, and re-layouts  57.7 us (20%)
  starting transfers between devices  37.1 us (13%)
  other arithmetic  33 us (12%)
  waiting for transfers between devices  23.5 us (8%)
  matrix products  22.9 us (8%)
    all_gather x8, blocking collectives, over_axes(): value = jnp.sum(lax.all_gather(value, axis), axis=0)  108 us
    reshape x1, local copies, waits for them, and re-layouts, average_cells(): view = fine_data.reshape(row_count * FIELDS * EDGE, 2, EDGE, 2 * PATCH)  27.2 us
    all_to_all x1, waiting for transfers between devices, shards(): lax.all_to_all(payload, ('gx', 'gy'), split_axis=0, concat_axis=0, tiled=...  23.5 us
    dot_general x1, matrix products, average_cells(): means = jnp.dot(pair_y.reshape(-1, PATCH), pairing, precision=HIGHEST)  17.3 us
    convert_element_type x2, local copies, waits for them, and re-layouts, average_cells(): return means.reshape(row_count, FIELDS, CELLS).astype(jnp.bfloat16)  17 us
    all_to_all x1, starting transfers between devices, shards(): lax.all_to_all(sent_snapshot, ('gx', 'gy'), split_axis=0, concat_axis=0,...  11.9 us
    all_to_all x1, starting transfers between devices, shards(): lax.all_to_all(payload, ('gx', 'gy'), split_axis=0, concat_axis=0, tiled=...  9.4 us
    ppermute x2, starting transfers between devices, extended(): lax.ppermute(last, axis, up)  8.2 us
  transfers between devices with their start and end apart: 8, of which 1 were waited for; matrix products, arithmetic and copies ran while one was open for 30% of the time, Pallas kernels for 0%

profile of v1, /device:TPU:1, one launch (start us, length us, event | category | flops | bytes accessed | tf_op | source)
XLA Modules:
  0.0 282.9 jit_solution(12297041739814382499)
XLA Ops:
  2.4 1.4 gather_fusion
  4.4 11.9 %all-to-all-start = ((s32[32,1,1]{2,1,0:T(1,128)}), s32[32,1,1]{2,1,0:T(1,128)S(1)}, u32[]{:S(2)}, u32[]{:S(2)}) async-start(s32[32,1,1]{2,1,0:T(1,128)} %copy.30), calls=%async_computation | async-start | bytes 32768 | tf_op jit(solution)/shard_map/all_to_all | solution.py:107
  16.3 27.2 %reshape.237 = bf16[2048,2,16,64]{3,2,1,0:T(8,128)(2,1)} reshape(bf16[32,4,32768]{2,1,0:T(4,128)(2,1)} %param.4) | data formatting | bytes 16777216 | tf_op jit(solution)/shard_map/reshape | solution.py:60
  43.6 6.9 %add_bitcast_fusion = f32[2048,16,64]{2,1,0:T(8,128)S(1)} fusion(bf16[2048,2,16,64]{3,2,1,0:T(8,128)(2,1)} %reshape.237), kind=kLoop, calls=%fused_computation.5 | loop fusion | flops 6291456 | bytes 16777216 | tf_op jit(solution)/shard_map/add | solution.py:61
  50.5 7.5 %slice_add_fusion = f32[2048,16,32]{2,1,0:T(8,128)} fusion(f32[2048,16,64]{2,1,0:T(8,128)S(1)} %add_bitcast_fusion), kind=kLoop, calls=%fused_computation.4 | loop fusion | flops 1048576 | bytes 12582912 | tf_op jit(solution)/shard_map/add | solution.py:62
  58.0 17.3 %convolution_convert_fusion = bf16[32768,16]{0,1:T(8,128)(2,1)S(1)} fusion(f32[32768,32]{1,0:T(8,128)} %bitcast.48, s32[32]{0:T(128)S(1)} %and_select_fusion), kind=kOutput, calls=%fused_computation.3 | convolution fusion | flops 201851904 | bytes 5243008 | tf_op jit(solution)/shard_map/dot_general | solution.py:67
  75.3 6.2 %copy.31 = bf16[32768,16]{1,0:T(8,128)(2,1)} copy(bf16[32768,16]{0,1:T(8,128)(2,1)S(1)} %convolution_convert_fusion) | data formatting | bytes 2097152 | tf_op jit(solution)/shard_map/convert_element_type | solution.py:68
  81.5 10.8 %convert_element_type.47 = bf16[32,4,4096]{2,1,0:T(4,128)(2,1)S(1)} reshape(bf16[32768,16]{1,0:T(8,128)(2,1)} %copy.31) | data formatting | bytes 2097152 | tf_op jit(solution)/shard_map/convert_element_type | solution.py:68
  92.2 1.4 gather_fusion.1
  93.7 1.6 broadcast_select_fusion
  95.3 9.4 %all-to-all-start.1 = ((bf16[32,4,4096]{2,1,0:T(4,128)(2,1)}), bf16[32,4,4096]{2,1,0:T(4,128)(2,1)S(1)}, u32[]{:S(2)}, u32[]{:S(2)}) async-start(bf16[32,4,4096]{2,1,0:T(4,128)(2,1)} %broadcast_select_fusion), calls=%async_computation.1 | async-start | bytes 2097152 | tf_op jit(solution)/shard_map/all_to_all | solution.py:106
  105.7 23.5 %all-to-all-done.1 = bf16[32,4,4096]{2,1,0:T(4,128)(2,1)S(1)} async-done(((bf16[32,4,4096]{2,1,0:T(4,128)(2,1)}), bf16[32,4,4096]{2,1,0:T(4,128)(2,1)S(1)}, u32[]{:S(2)}, u32[]{:S(2)}) %all-to-all-start.1) | async-done | bytes 1048608 | tf_op jit(solution)/shard_map/all_to_all | solution.py:106
  132.6 9.1 %all-gather = f32[256,64]{1,0:T(8,128)S(1)} all-gather(f32[64,64]{1,0:T(8,128)S(1)} %fusion.30), channel_id=2, replica_groups=mesh['gx'=4,'gy'=8,'gz_0'=4,'gz_1'=2] {'gx'}, dimensions={0}, use_global_device_ids=true | all-gather | bytes 81920 | tf_op jit(solution)/shard_map/all_gather | solution.py:54
  141.7 19.7 %all-gather.1 = f32[512,64]{1,0:T(8,128)S(1)} all-gather(f32[64,64]{1,0:T(8,128)S(1)} %reduce_sum.111), channel_id=3, replica_groups=mesh['gx'=4,'gy'=8,'gz_0'=4,'gz_1'=2] {'gy'}, dimensions={0}, use_global_device_ids=true | all-gather | bytes 147456 | tf_op jit(solution)/shard_map/all_gather | solution.py:54
  161.4 9.9 %all-gather.2 = f32[256,64]{1,0:T(8,128)S(1)} all-gather(f32[64,64]{1,0:T(8,128)S(1)} %reduce_sum.112), channel_id=4, replica_groups=mesh['gx'=4,'gy'=8,'gz_0'=4,'gz_1'=2] {'gz_0'}, dimensions={0}, use_global_device_ids=true | all-gather | bytes 81920 | tf_op jit(solution)/shard_map/all_gather | solution.py:54
  171.4 17.3 %all-gather.3 = f32[128,64]{1,0:T(8,128)S(1)} all-gather(f32[64,64]{1,0:T(8,128)S(1)} %reduce_sum.113), channel_id=5, replica_groups=mesh['gx'=4,'gy'=8,'gz_0'=4,'gz_1'=2] {'gz_1'}, dimensions={0}, use_global_device_ids=true | all-gather | bytes 49152 | tf_op jit(solution)/shard_map/all_gather | solution.py:54
  188.9 5.8 %cholesky.16 = f32[64,64]{1,0:T(8,128)S(1)} custom-call(f32[64,64]{1,0:T(8,128)S(1)} %fusion.11), custom_call_target="Cholesky" | custom-call | tf_op jit(solution)/shard_map/jit(cholesky)/cholesky | solution.py:78
  196.1 4.9 %custom-call.6 = f32[1,64,64]{1,2,0:T(8,128)S(1)} custom-call(f32[1,64,64]{2,1,0:T(8,128)S(1)} %fusion.8), custom_call_target="InvertDiagBlocksLowerTriangular" | custom-call | tf_op jit(solution)/shard_map/triangular_solve | solution.py:79
  201.0 3.1 %collective-permute-start.4 = (bf16[16,16,64]{2,1,0:T(8,128)(2,1)S(1)}, bf16[16,16,64]{2,1,0:T(8,128)(2,1)S(1)}, u32[]{:S(2)}, u32[]{:S(2)}) collective-permute-start(bf16[16,16,64]{2,1,0:T(8,128)(2,1)S(1)} %get-tuple-element.29), channel_id=1, source_target_pairs={{0,1},{1,2},{2,3},{3,4},{4,5},{5,6},{6,7},{8,9},{9,10},{10,11},{11... | collective-permute-start | bytes 98312 | tf_op jit(solution)/shard_map/ppermute | solution.py:46
  204.1 1.9 collective-permute-start.5
  206.0 1.3 collective-permute-start.3
  207.3 4.0 %collective-permute-start = (bf16[16,1,1024]{2,1,0:T(2,128)(2,1)S(1)}, bf16[16,1,1024]{2,1,0:T(2,128)(2,1)S(1)}, u32[]{:S(2)}, u32[]{:S(2)}) collective-permute-start(bf16[16,1,1024]{2,1,0:T(2,128)(2,1)S(1)} %get-tuple-element.26), channel_id=1, source_target_pairs={{0,8},{8,16},{16,24},{24,32},{32,40},{40,48},{48,56},{1,9},{9,17},... | collective-permute-start | bytes 98312 | tf_op jit(solution)/shard_map/ppermute | solution.py:27
  213.1 4.2 %collective-permute-start.1 = (bf16[1,16,1024]{2,1,0:T(8,128)(2,1)S(1)}, bf16[1,16,1024]{2,1,0:T(8,128)(2,1)S(1)}, u32[]{:S(2)}, u32[]{:S(2)}) collective-permute-start(bf16[1,16,1024]{2,1,0:T(8,128)(2,1)S(1)} %slice.70), channel_id=1, source_target_pairs={{0,64},{64,128},{128,192},{1,65},{65,129},{129,193},{2,66},{66,130... | collective-permute-start | bytes 98312 | tf_op jit(solution)/shard_map/ppermute | solution.py:27
  218.9 1.7 convert_element_type.49
  221.8 1.4 fusion.2
  223.2 1.7 reshape.240
  224.9 2.3 convolution_convert_fusion.1
  228.5 1.7 convert_element_type.54
  230.3 9.1 %all-gather.4 = f32[256,64]{1,0:T(8,128)S(1)} all-gather(f32[64,64]{1,0:T(8,128)S(1)} %fusion.31), channel_id=6, replica_groups=mesh['gx'=4,'gy'=8,'gz_0'=4,'gz_1'=2] {'gx'}, dimensions={0}, use_global_device_ids=true | all-gather | bytes 81920 | tf_op jit(solution)/shard_map/all_gather | solution.py:54
  239.4 18.4 %all-gather.5 = f32[512,64]{1,0:T(8,128)S(1)} all-gather(f32[64,64]{1,0:T(8,128)S(1)} %reduce_sum.115), channel_id=7, replica_groups=mesh['gx'=4,'gy'=8,'gz_0'=4,'gz_1'=2] {'gy'}, dimensions={0}, use_global_device_ids=true | all-gather | bytes 147456 | tf_op jit(solution)/shard_map/all_gather | solution.py:54
  257.8 9.1 %all-gather.6 = f32[256,64]{1,0:T(8,128)S(1)} all-gather(f32[64,64]{1,0:T(8,128)S(1)} %reduce_sum.116), channel_id=8, replica_groups=mesh['gx'=4,'gy'=8,'gz_0'=4,'gz_1'=2] {'gz_0'}, dimensions={0}, use_global_device_ids=true | all-gather | bytes 81920 | tf_op jit(solution)/shard_map/all_gather | solution.py:54
  267.0 15.0 %all-gather.7 = f32[128,64]{1,0:T(8,128)S(1)} all-gather(f32[64,64]{1,0:T(8,128)S(1)} %reduce_sum.117), channel_id=9, replica_groups=mesh['gx'=4,'gy'=8,'gz_0'=4,'gz_1'=2] {'gz_1'}, dimensions={0}, use_global_device_ids=true | all-gather | bytes 49152 | tf_op jit(solution)/shard_map/all_gather | solution.py:54
  (77 shorter events, 15.1 us)
Async XLA Ops:
  0.6 212.1 %copy-start = (f32[64,32]{0,1:T(8,128)S(1)}, f32[64,32]{0,1:T(8,128)}, u32[]{:S(2)}) copy-start(f32[64,32]{0,1:T(8,128)} %param.7) | copy-start | bytes 24580
  4.4 90.8 %all-to-all-start = ((s32[32,1,1]{2,1,0:T(1,128)}), s32[32,1,1]{2,1,0:T(1,128)S(1)}, u32[]{:S(2)}, u32[]{:S(2)}) async-start(s32[32,1,1]{2,1,0:T(1,128)} %copy.30), calls=%async_computation | async-start | bytes 32768 | tf_op jit(solution)/shard_map/all_to_all | solution.py:107
  95.3 33.9 %all-to-all-start.1 = ((bf16[32,4,4096]{2,1,0:T(4,128)(2,1)}), bf16[32,4,4096]{2,1,0:T(4,128)(2,1)S(1)}, u32[]{:S(2)}, u32[]{:S(2)}) async-start(bf16[32,4,4096]{2,1,0:T(4,128)(2,1)} %broadcast_select_fusion), calls=%async_computation.1 | async-start | bytes 2097152 | tf_op jit(solution)/shard_map/all_to_all | solution.py:106
  105.6 25.4 %copy-start.4 = (pred[64]{0:T(512)(128)(4,1)}, pred[64]{0:T(512)(128)(4,1)S(1)}, u32[]{:S(2)}) copy-start(pred[64]{0:T(512)(128)(4,1)S(1)} %broadcast_in_dim.95) | copy-start | bytes 196
  131.1 1.1 copy-start.1
  132.2 85.1 %copy-start.2 = (bf16[64,4096]{0,1:T(8,128)(2,1)S(1)}, bf16[64,4096]{0,1:T(8,128)(2,1)}, u32[]{:S(2)}) copy-start(bf16[64,4096]{0,1:T(8,128)(2,1)} %copy-done.1) | copy-start | bytes 1572868
  132.2 85.1 %copy-start.5 = (pred[64]{0:T(512)(128)(4,1)S(1)}, pred[64]{0:T(512)(128)(4,1)}, u32[]{:S(2)}) copy-start(pred[64]{0:T(512)(128)(4,1)} %copy-done.4) | copy-start | bytes 196
  188.8 31.8 %copy-start.3 = (f32[64,64]{1,0:T(8,128)}, f32[64,64]{1,0:T(8,128)S(1)}, u32[]{:S(2)}) copy-start(f32[64,64]{1,0:T(8,128)S(1)} %copy.38) | copy-start | bytes 49156
  201.0 12.1 %collective-permute-start.4 = (bf16[16,16,64]{2,1,0:T(8,128)(2,1)S(1)}, bf16[16,16,64]{2,1,0:T(8,128)(2,1)S(1)}, u32[]{:S(2)}, u32[]{:S(2)}) collective-permute-start(bf16[16,16,64]{2,1,0:T(8,128)(2,1)S(1)} %get-tuple-element.29), channel_id=1, source_target_pairs={{0,1},{1,2},{2,3},{3,4},{4,5},{5,6},{6,7},{8,9},{9,10},{10,11},{11... | collective-permute-start | bytes 98312 | tf_op jit(solution)/shard_map/ppermute | solution.py:46
  204.1 16.5 %collective-permute-start.5 = (bf16[16,16,64]{2,1,0:T(8,128)(2,1)S(1)}, bf16[16,16,64]{2,1,0:T(8,128)(2,1)S(1)}, u32[]{:S(2)}, u32[]{:S(2)}) collective-permute-start(bf16[16,16,64]{2,1,0:T(8,128)(2,1)S(1)} %get-tuple-element.28), channel_id=1, source_target_pairs={{1,0},{2,1},{3,2},{4,3},{5,4},{6,5},{7,6},{9,8},{10,9},{11,10},{12... | collective-permute-start | bytes 98312 | tf_op jit(solution)/shard_map/ppermute | solution.py:47
  206.0 15.3 %collective-permute-start.3 = (bf16[16,1,1024]{2,1,0:T(2,128)(2,1)S(1)}, bf16[16,1,1024]{2,1,0:T(2,128)(2,1)S(1)}, u32[]{:S(2)}, u32[]{:S(2)}) collective-permute-start(bf16[16,1,1024]{2,1,0:T(2,128)(2,1)S(1)} %get-tuple-element.27), channel_id=1, source_target_pairs={{8,0},{16,8},{24,16},{32,24},{40,32},{48,40},{56,48},{9,1},{17,9},... | collective-permute-start | bytes 98312 | tf_op jit(solution)/shard_map/ppermute | solution.py:28
  207.3 14.0 %collective-permute-start = (bf16[16,1,1024]{2,1,0:T(2,128)(2,1)S(1)}, bf16[16,1,1024]{2,1,0:T(2,128)(2,1)S(1)}, u32[]{:S(2)}, u32[]{:S(2)}) collective-permute-start(bf16[16,1,1024]{2,1,0:T(2,128)(2,1)S(1)} %get-tuple-element.26), channel_id=1, source_target_pairs={{0,8},{8,16},{16,24},{24,32},{32,40},{40,48},{48,56},{1,9},{9,17},... | collective-permute-start | bytes 98312 | tf_op jit(solution)/shard_map/ppermute | solution.py:27
  211.5 9.9 %collective-permute-start.2 = (bf16[1,16,1024]{2,1,0:T(8,128)(2,1)S(1)}, bf16[1,16,1024]{2,1,0:T(8,128)(2,1)S(1)}, u32[]{:S(2)}, u32[]{:S(2)}) collective-permute-start(bf16[1,16,1024]{2,1,0:T(8,128)(2,1)S(1)} %slice.72), channel_id=1, source_target_pairs={{64,0},{128,64},{192,128},{65,1},{129,65},{193,129},{66,2},{130,66... | collective-permute-start | bytes 98312 | tf_op jit(solution)/shard_map/ppermute | solution.py:28
  213.1 8.3 %collective-permute-start.1 = (bf16[1,16,1024]{2,1,0:T(8,128)(2,1)S(1)}, bf16[1,16,1024]{2,1,0:T(8,128)(2,1)S(1)}, u32[]{:S(2)}, u32[]{:S(2)}) collective-permute-start(bf16[1,16,1024]{2,1,0:T(8,128)(2,1)S(1)} %slice.70), channel_id=1, source_target_pairs={{0,64},{64,128},{128,192},{1,65},{65,129},{129,193},{2,66},{66,130... | collective-permute-start | bytes 98312 | tf_op jit(solution)/shard_map/ppermute | solution.py:27
